TPU v7x, 32 devices: a whole 2x2x4 slice. The times are simulated.
32 devices in a mesh: rep: 8 (over z, core), rows: 4 (over y, x).
Axes of the slice: x: 2, y: 2, z: 4, core: 2. Of those that a mesh axis runs over, the one named last changes fastest.
Arguments:
- weights: bfloat16 [7168, 2048], P('rows'), may hold values from -6 to 6
- momentum: float32 [8, 7168, 2048], P('rep', 'rows'), may hold values from -8 to 8
- gradient: bfloat16 [8, 7168, 2048], P('rep', 'rows'), may hold values from -8 to 8
- right_factor: float32 [2048, 512], P('rows'), may hold values from -6 to 6
Outputs:
- new_weights: bfloat16 [7168, 2048], P('rows')
- new_momentum: float32 [8, 7168, 2048], P('rep', 'rows')
- new_right: float32 [2048, 512], P('rows')
All inputs are finite; a program needn't handle non-finite values.
Results may differ from a plain program's by a relative error of at most 0.019.
Values may be sent and summed in bfloat16 or wider, within the bound.
A program may use at most 128 MiB of HBM per device.

v0:
```python
import jax
import jax.numpy as jnp
from jax import lax
from jax.sharding import PartitionSpec as P

M = 7168
N = 2048
momentum_keep = 0.05
learn_rate = 0.5
tiny = 1e-06


def per_device(weights, momentum, gradient, right_factor):
    groups = lax.axis_size("rep")
    shards = lax.axis_size("rows")
    combined = momentum[0] + gradient[0].astype(jnp.float32)
    combined_half = combined.astype(jnp.bfloat16)
    columns = combined.shape[1]
    share = columns // shards
    left_local = jnp.dot(
        combined_half,
        lax.all_gather(right_factor.astype(jnp.bfloat16), "rows", axis=0, tiled=True),
        preferred_element_type=jnp.float32,
    )
    left_local = lax.optimization_barrier(left_local.astype(jnp.bfloat16)).astype(jnp.float32)
    left_mean = lax.psum(left_local.astype(jnp.bfloat16), "rep").astype(jnp.float32) / groups
    gram = lax.psum(jnp.dot(left_mean.T, left_mean, precision=lax.Precision.HIGHEST), "rows")
    chol = jnp.linalg.cholesky(gram)
    left_orth = jax.scipy.linalg.solve_triangular(chol, left_mean.T, lower=True).T
    left_half = left_orth.astype(jnp.bfloat16)
    partial_right = jnp.einsum(
        "ij,ik->jk", combined_half, left_half, preferred_element_type=jnp.float32
    )
    right_mean = lax.psum(partial_right, ("rep", "rows")) / groups
    normed = right_mean / jnp.sqrt(jnp.mean(right_mean * right_mean, axis=0) + tiny)
    feedback = jnp.dot(
        left_half, right_mean.astype(jnp.bfloat16).T, preferred_element_type=jnp.float32
    )
    update = jnp.dot(left_half, normed.astype(jnp.bfloat16).T, preferred_element_type=jnp.float32)
    new_right = lax.dynamic_slice_in_dim(normed, lax.axis_index("rows") * share, share, 0)
    new_momentum = combined - momentum_keep * feedback
    new_weights = (weights.astype(jnp.float32) - learn_rate * jnp.sqrt(M / N) * update).astype(
        jnp.bfloat16
    )
    return (new_weights, new_momentum[None], new_right)


def solution(mesh):
    in_specs = (P("rows", None), P("rep", "rows", None), P("rep", "rows", None), P("rows", None))
    out_specs = (P("rows", None), P("rep", "rows", None), P("rows", None))
    return jax.shard_map(
        per_device, mesh=mesh, in_specs=in_specs, out_specs=out_specs, check_vma=False
    )
```

profile of v0, /device:TPU:0, one launch (start us, length us, event | category | flops | bytes accessed | tf_op | source)
XLA Modules:
  0.0 525.9 jit_solution(10342217912073874617)
XLA Ops:
  9.4 39.0 %all-gather.2.cloned.1.call-done = bf16[2048,512]{1,0:T(8,128)(2,1)} async-done(((bf16[512,512]{1,0:T(8,128)(2,1)}), bf16[2048,512]{1,0:T(8,128)(2,1)}) %all-gather.2.cloned.1.call-update) | async-done | bytes 2097168 | tf_op jit(solution)/shard_map/all_gather | solution.py:22
  48.3 13.1 %convolution_convert_fusion = bf16[1792,512]{1,0:T(8,128)(2,1)} fusion(bf16[2048,512]{1,0:T(8,128)(2,1)} %all-gather.2.cloned.1.call-done, f32[1,1792,2048]{2,1,0:T(8,128)} %param.5, bf16[1,1792,2048]{2,1,0:T(8,128)(2,1)} %param.6), kind=kOutput, calls=%fused_computation.13 | convolution fusion | flops 3770023936 | bytes 25952256 | tf_op jit(solution)/shard_map/dot_general | solution.py:20
  61.5 63.3 %all-reduce.5.cloned.1.call-done = bf16[1792,512]{1,0:T(8,128)(2,1)} async-done(((bf16[1792,512]{1,0:T(8,128)(2,1)}), bf16[1792,512]{1,0:T(8,128)(2,1)}) %all-reduce.5.cloned.1.call-update) | async-done | bytes 1835024 | tf_op jit(solution)/shard_map/psum | solution.py:26
  124.7 9.4 %fusion.2 = f32[512,512]{0,1:T(8,128)} fusion(bf16[1792,512]{1,0:T(8,128)(2,1)} %all-reduce.5.cloned.1.call-done), kind=kOutput, calls=%fused_computation.12 | convolution fusion | flops 5638979584 | bytes 2883584 | tf_op jit(solution)/shard_map/dot_general | solution.py:27
  134.4 2.4 fusion.1
  136.8 50.0 %all-reduce.7.cloned.1.call-done = f32[512,512]{0,1:T(8,128)} async-done(((f32[512,512]{0,1:T(8,128)}), f32[512,512]{0,1:T(8,128)}) %all-reduce.7.cloned.1.call-update) | async-done | bytes 1048592 | tf_op jit(solution)/shard_map/psum | solution.py:27
  189.8 11.7 %cholesky.104 = f32[128,128]{1,0:T(8,128)S(1)} custom-call(f32[128,128]{1,0:T(8,128)S(1)} %cholesky.266), custom_call_target="Cholesky" | custom-call | tf_op jit(solution)/shard_map/jit(cholesky)/cholesky | solution.py:28
  201.5 9.8 %custom-call.31 = f32[1,128,128]{1,2,0:T(8,128)S(1)} custom-call(f32[1,128,128]{2,1,0:T(8,128)S(1)} %get-tuple-element.30), custom_call_target="InvertDiagBlocksLowerTriangular" | custom-call | tf_op jit(solution)/shard_map/jit(cholesky)/cholesky | solution.py:28
  212.2 11.7 %cholesky.217 = f32[128,128]{1,0:T(8,128)S(1)} custom-call(f32[128,128]{1,0:T(8,128)S(1)} %cholesky.270), custom_call_target="Cholesky" | custom-call | tf_op jit(solution)/shard_map/jit(cholesky)/cholesky | solution.py:28
  223.9 10.2 %custom-call.32 = f32[1,128,128]{1,2,0:T(8,128)S(1)} custom-call(f32[1,128,128]{2,1,0:T(8,128)S(1)} %get-tuple-element.27), custom_call_target="InvertDiagBlocksLowerTriangular" | custom-call | tf_op jit(solution)/shard_map/jit(cholesky)/cholesky | solution.py:28
  234.8 11.7 %cholesky.238 = f32[128,128]{1,0:T(8,128)S(1)} custom-call(f32[128,128]{1,0:T(8,128)S(1)} %cholesky.275), custom_call_target="Cholesky" | custom-call | tf_op jit(solution)/shard_map/jit(cholesky)/cholesky | solution.py:28
  247.3 9.8 %custom-call.33 = f32[1,128,128]{1,2,0:T(8,128)S(1)} custom-call(f32[1,128,128]{2,1,0:T(8,128)S(1)} %get-tuple-element.24), custom_call_target="InvertDiagBlocksLowerTriangular" | custom-call | tf_op jit(solution)/shard_map/jit(cholesky)/cholesky | solution.py:28
  257.7 11.9 %cholesky.255 = f32[128,128]{1,0:T(8,128)S(1)} custom-call(f32[128,128]{1,0:T(8,128)S(1)} %convolution_subtract_fusion.4), custom_call_target="Cholesky" | custom-call | tf_op jit(solution)/shard_map/jit(cholesky)/cholesky | solution.py:28
  273.6 8.5 %while.1 = (s32[]{:T(128)}, f32[512,512]{1,0:T(8,128)S(1)}, s32[4,2]{0,1:T(2,128)S(1)}, f32[4,128,128]{2,1,0:T(8,128)S(1)}, s32[]{:T(128)}) while((s32[]{:T(128)}, f32[512,512]{1,0:T(8,128)S(1)}, s32[4,2]{0,1:T(2,128)S(1)}, f32[4,128,128]{2,1,0:T(8,128)S(1)}, s32[]{:T(128)}) %tuple.34), condition=%wide.while_cond, body=%wide.while_body.sunk | while | flops 2 | bytes 131181 | solution.py:29
  282.1 39.3 %custom-call.34 = f32[4,128,128]{1,2,0:T(8,128)S(1)} custom-call(f32[4,128,128]{2,1,0:T(8,128)S(1)} %get-tuple-element.10), custom_call_target="InvertDiagBlocksLowerTriangular" | custom-call | tf_op jit(solution)/shard_map/jit(_solve_triangular)/triangular_solve | solution.py:29
  321.4 2.3 fusion.45
  323.7 2.8 convolution_subtract_fusion.1
  327.5 3.2 convolution_subtract_fusion
  331.7 4.7 fusion.9
  338.3 11.3 %fusion.41 = f32[2048,512]{1,0:T(8,128)} fusion(f32[1,1792,2048]{2,1,0:T(8,128)} %param.5, bf16[1,1792,2048]{2,1,0:T(8,128)(2,1)S(1)} %bitcast.67, bf16[128,1792]{1,0:T(8,128)(2,1)S(1)} %convolution_convert_fusion.1, bf16[128,1792]{1,0:T(8,128)(2,1)S(1)} %get-tuple-element.33, bf16[128,1792]{1,0:T(8,128)(2,1)S(1)} %get-tuple-element.35, ...), kind=kOutput, calls=%fused_computation.86 | convolution fusion | flops 3776446464 | bytes 28049408 | tf_op jit(solution)/shard_map/ij,ik->jk/dot_general | solution.py:31
  349.6 142.5 %all-reduce.9.cloned.1.call-done = f32[2048,512]{1,0:T(8,128)} async-done(((f32[2048,512]{1,0:T(8,128)}), f32[2048,512]{1,0:T(8,128)}) %all-reduce.9.cloned.1.call-update) | async-done | bytes 4194320 | tf_op jit(solution)/shard_map/psum | solution.py:34
  492.1 2.9 multiply_reduce_fusion
  496.7 8.2 %subtract_convert_fusion = bf16[1792,2048]{1,0:T(8,128)(2,1)} fusion(bf16[1792,2048]{1,0:T(8,128)(2,1)} %param.4, f32[2048,512]{1,0:T(8,128)S(1)} %multiply_divide_fusion, bf16[128,1792]{1,0:T(8,128)(2,1)S(1)} %copy-done.6, bf16[128,1792]{1,0:T(8,128)(2,1)S(1)} %copy-done.4, bf16[128,1792]{1,0:T(8,128)(2,1)S(1)} %get-tuple-element.35, ...), kind=kOutput, calls=%fused_computation.5 | convolution fusion | flops 3781165056 | bytes 20709376 | tf_op jit(solution)/shard_map/dot_general | solution.py:39
  506.0 13.0 %fusion = f32[1,1792,2048]{2,1,0:T(8,128)} fusion(f32[1,1792,2048]{2,1,0:T(8,128)} %param.5, bf16[1,1792,2048]{2,1,0:T(8,128)(2,1)} %param.6, f32[2048,512]{1,0:T(8,128)S(1)} %copy-done, bf16[128,1792]{1,0:T(8,128)(2,1)} %copy-done.5, bf16[128,1792]{1,0:T(8,128)(2,1)} %copy-done.3, bf16[128,1792]{1,0:T(8,128)(2,1)S(1)} %get-tuple-element.35, ...), kind=kOutput, calls=%fused_computation.4 | convolution fusion | flops 3782213632 | bytes 42729472 | tf_op jit(solution)/shard_map/dot_general | solution.py:36
  (69 shorter events, 24.9 us)
Async XLA Ops:
  7.2 41.2 %all-gather.2.cloned.1.call-start = ((), (), s32[]{:S(2)}) async-start(), calls=%async_computation | async-start | bytes 2621440 | tf_op jit(solution)/shard_map/all_gather | solution.py:22
  9.3 115.4 %all-reduce.5.cloned.1.call-start = ((), (), s32[]{:S(2)}) async-start(), calls=%async_computation.1 | async-start | bytes 3670016 | tf_op jit(solution)/shard_map/psum | solution.py:26
  61.4 125.4 %all-reduce.7.cloned.1.call-start = ((), (), s32[]{:S(2)}) async-start(), calls=%async_computation.2 | async-start | bytes 2097152 | tf_op jit(solution)/shard_map/psum | solution.py:27
  124.7 9.7 %copy-start.2 = (bf16[1792,512]{1,0:T(8,128)(2,1)S(1)}, bf16[1792,512]{1,0:T(8,128)(2,1)}, u32[]{:S(2)}) copy-start(bf16[1792,512]{1,0:T(8,128)(2,1)} %all-reduce.5.cloned.1.call-done) | copy-start | bytes 5505028
  134.1 358.0 %all-reduce.9.cloned.1.call-start = ((), (), s32[]{:S(2)}) async-start(), calls=%async_computation.3 | async-start | bytes 8388608 | tf_op jit(solution)/shard_map/psum | solution.py:34
  321.4 6.1 %copy-start.1 = (f32[512,1792]{0,1:T(8,128)S(1)}, f32[512,1792]{0,1:T(8,128)}, u32[]{:S(2)}) copy-start(f32[512,1792]{0,1:T(8,128)} %fusion.1) | copy-start | bytes 11010052
  326.5 11.8 %slice-start = ((s8[7340032]{0:T(1024)(128)(4,1)}), s8[4194304]{0:T(1024)(128)(4,1)S(1)}, s32[]{:S(2)}) async-start(s8[7340032]{0:T(1024)(128)(4,1)} %bitcast.66), calls=%async_computation.4 | async-start | bytes 8388608
  330.7 7.6 %slice-start.1 = ((s8[7340032]{0:T(1024)(128)(4,1)}), s8[3145728]{0:T(1024)(128)(4,1)S(1)}, s32[]{:S(2)}) async-start(s8[7340032]{0:T(1024)(128)(4,1)} %bitcast.66), calls=%async_computation.5 | async-start | bytes 6291456
  331.7 17.9 %copy-start.3 = (bf16[128,1792]{1,0:T(8,128)(2,1)}, bf16[128,1792]{1,0:T(8,128)(2,1)S(1)}, u32[]{:S(2)}) copy-start(bf16[128,1792]{1,0:T(8,128)(2,1)S(1)} %get-tuple-element.33) | copy-start | bytes 1376260
  337.5 0.8 copy-start.5
  492.1 3.4 copy-start
  495.6 1.0 copy-start.4
  495.6 1.2 copy-start.6
Sparse Core Ops, SparseCore 0:
  10.4 37.8 all-gather.1
  61.5 63.1 all-reduce.4
  134.3 52.4 all-reduce.6
  349.7 142.3 all-reduce.8
where the time goes:
time: 534 us; the launch traced here: 526 us
  waiting for transfers between devices  295 us (55%)
  other arithmetic  128 us (24%)
  matrix products  72.8 us (14%)
  between operations  17 us (3%)
  local copies, waits for them, and re-layouts  13.1 us (2%)
    psum x1, waiting for transfers between devices, per_device(): right_mean = lax.psum(partial_right, ('rep', 'rows')) / groups  143 us
    another operation x14, other arithmetic, per_device(): chol = jnp.linalg.cholesky(gram)  79 us
    psum x1, waiting for transfers between devices, per_device(): lax.psum(left_local.astype(jnp.bfloat16), 'rep').astype(jnp.float32)  63.3 us
    psum x1, waiting for transfers between devices, per_device(): lax.psum(jnp.dot(left_mean.T, left_mean, precision=lax.Precision.HIGHEST)...  50 us
    another operation x3, other arithmetic, per_device(): jax.scipy.linalg.solve_triangular(chol, left_mean.T, lower=True)  39.4 us
    all_gather x1, waiting for transfers between devices, per_device(): lax.all_gather(right_factor.astype(jnp.bfloat16), 'rows', axis=0, tiled=T...  39 us
    another operation x7, matrix products, per_device(): jax.scipy.linalg.solve_triangular(chol, left_mean.T, lower=True)  16 us
    dot_general x1, matrix products, per_device(): jnp.dot(combined_half, lax.all_gather(right_factor.astype(jnp.bfloat16),...  13.1 us
  transfers between devices with their start and end apart: 4, of which 4 were waited for; matrix products, arithmetic and copies ran while one was open for 0% of the time, Pallas kernels for 0%

commit v1 on v0

--- a/solution.py
+++ b/solution.py
@@ -23,7 +23,10 @@
         preferred_element_type=jnp.float32,
     )
     left_local = lax.optimization_barrier(left_local.astype(jnp.bfloat16)).astype(jnp.float32)
-    left_mean = lax.psum(left_local.astype(jnp.bfloat16), "rep").astype(jnp.float32) / groups
+    left_mean = (
+        jnp.sum(lax.all_gather(left_local.astype(jnp.bfloat16), "rep"), axis=0).astype(jnp.float32)
+        / groups
+    )
     gram = lax.psum(jnp.dot(left_mean.T, left_mean, precision=lax.Precision.HIGHEST), "rows")
     chol = jnp.linalg.cholesky(gram)
     left_orth = jax.scipy.linalg.solve_triangular(chol, left_mean.T, lower=True).T

time: 534 us -> 605 us (1.13)
  waiting for transfers between devices: 295 us -> 363 us
  other arithmetic: 128 us -> 136 us
    all_gather x0 -> x1, waiting for transfers between devices: none -> 134 us  [per_device(): lax.all_gather(left_local.astype(jnp.bfloat16), 'rep')]
    psum x1 -> x0, waiting for transfers between devices: 63.3 us -> none  [per_device(): lax.psum(left_local.astype(jnp.bfloat16), 'rep').astype(jnp.float32)]
    reduce_sum x0 -> x1, other arithmetic: none -> 8.52 us  [per_device(): jnp.sum(lax.all_gather(left_local.astype(jnp.bfloat16), 'rep'), axis=0)]
where the time goes in v1:
time: 605 us; the launch traced here: 601 us
  waiting for transfers between devices  363 us (60%)
  other arithmetic  136 us (22%)
  matrix products  70.6 us (12%)
  between operations  16.8 us (3%)
  local copies, waits for them, and re-layouts  13.1 us (2%)
    psum x1, waiting for transfers between devices, per_device(): right_mean = lax.psum(partial_right, ('rep', 'rows')) / groups  143 us
    all_gather x1, waiting for transfers between devices, per_device(): lax.all_gather(left_local.astype(jnp.bfloat16), 'rep')  134 us
    another operation x14, other arithmetic, per_device(): chol = jnp.linalg.cholesky(gram)  79 us
    psum x1, waiting for transfers between devices, per_device(): lax.psum(jnp.dot(left_mean.T, left_mean, precision=lax.Precision.HIGHEST)...  48.2 us
    another operation x3, other arithmetic, per_device(): jax.scipy.linalg.solve_triangular(chol, left_mean.T, lower=True)  39.4 us
    all_gather x1, waiting for transfers between devices, per_device(): lax.all_gather(right_factor.astype(jnp.bfloat16), 'rows', axis=0, tiled=T...  39 us
    another operation x7, matrix products, per_device(): jax.scipy.linalg.solve_triangular(chol, left_mean.T, lower=True)  16 us
    dot_general x1, matrix products, per_device(): jnp.dot(combined_half, lax.all_gather(right_factor.astype(jnp.bfloat16),...  13.1 us
  transfers between devices with their start and end apart: 4, of which 4 were waited for; matrix products, arithmetic and copies ran while one was open for 0% of the time, Pallas kernels for 0%

profile of v1, /device:TPU:0, one launch (start us, length us, event | category | flops | bytes accessed | tf_op | source)
XLA Modules:
  0.0 601.0 jit_solution(4330169185956516917)
XLA Ops:
  9.4 39.0 %all-gather.4.cloned.1.call-done = bf16[2048,512]{1,0:T(8,128)(2,1)} async-done(((bf16[512,512]{1,0:T(8,128)(2,1)}), bf16[2048,512]{1,0:T(8,128)(2,1)}) %all-gather.4.cloned.1.call-update) | async-done | bytes 2097168 | tf_op jit(solution)/shard_map/all_gather | solution.py:22
  48.3 13.1 %convolution_convert_fusion = bf16[1792,512]{1,0:T(8,128)(2,1)} fusion(bf16[2048,512]{1,0:T(8,128)(2,1)} %all-gather.4.cloned.1.call-done, f32[1,1792,2048]{2,1,0:T(8,128)} %param.5, bf16[1,1792,2048]{2,1,0:T(8,128)(2,1)} %param.6), kind=kOutput, calls=%fused_computation.13 | convolution fusion | flops 3770023936 | bytes 25952256 | tf_op jit(solution)/shard_map/dot_general | solution.py:20
  61.9 133.5 %all-gather.6.cloned.1.call-done = bf16[14336,512]{1,0:T(8,128)(2,1)} async-done(((bf16[1792,512]{1,0:T(8,128)(2,1)}), bf16[14336,512]{1,0:T(8,128)(2,1)}) %all-gather.6.cloned.1.call-update) | async-done | bytes 14680080 | tf_op jit(solution)/shard_map/all_gather | solution.py:27
  195.5 8.5 %reduce_sum.21 = bf16[1792,512]{1,0:T(8,128)(2,1)S(1)} reduce(bf16[8,1792,512]{2,1,0:T(8,128)(2,1)} %bitcast.67, bf16[]{:T(256)} %constant.155.clone.1), dimensions={0}, to_apply=%region_0.0 | reduce | flops 6422528 | bytes 16515074 | tf_op jit(solution)/shard_map/reduce_sum | solution.py:27
  204.0 7.2 %fusion.2 = f32[512,512]{0,1:T(8,128)} fusion(bf16[1792,512]{1,0:T(8,128)(2,1)S(1)} %reduce_sum.21), kind=kOutput, calls=%fused_computation.12 | convolution fusion | flops 5638979584 | bytes 2883584 | tf_op jit(solution)/shard_map/dot_general | solution.py:30
  211.4 2.4 fusion.1
  213.8 48.2 %all-reduce.4.cloned.1.call-done = f32[512,512]{0,1:T(8,128)} async-done(((f32[512,512]{0,1:T(8,128)}), f32[512,512]{0,1:T(8,128)}) %all-reduce.4.cloned.1.call-update) | async-done | bytes 1048592 | tf_op jit(solution)/shard_map/psum | solution.py:30
  265.0 11.7 %cholesky.104 = f32[128,128]{1,0:T(8,128)S(1)} custom-call(f32[128,128]{1,0:T(8,128)S(1)} %cholesky.266), custom_call_target="Cholesky" | custom-call | tf_op jit(solution)/shard_map/jit(cholesky)/cholesky | solution.py:31
  276.7 9.8 %custom-call.31 = f32[1,128,128]{1,2,0:T(8,128)S(1)} custom-call(f32[1,128,128]{2,1,0:T(8,128)S(1)} %get-tuple-element.30), custom_call_target="InvertDiagBlocksLowerTriangular" | custom-call | tf_op jit(solution)/shard_map/jit(cholesky)/cholesky | solution.py:31
  287.3 11.7 %cholesky.217 = f32[128,128]{1,0:T(8,128)S(1)} custom-call(f32[128,128]{1,0:T(8,128)S(1)} %cholesky.270), custom_call_target="Cholesky" | custom-call | tf_op jit(solution)/shard_map/jit(cholesky)/cholesky | solution.py:31
  299.1 10.2 %custom-call.32 = f32[1,128,128]{1,2,0:T(8,128)S(1)} custom-call(f32[1,128,128]{2,1,0:T(8,128)S(1)} %get-tuple-element.27), custom_call_target="InvertDiagBlocksLowerTriangular" | custom-call | tf_op jit(solution)/shard_map/jit(cholesky)/cholesky | solution.py:31
  310.0 11.7 %cholesky.238 = f32[128,128]{1,0:T(8,128)S(1)} custom-call(f32[128,128]{1,0:T(8,128)S(1)} %cholesky.275), custom_call_target="Cholesky" | custom-call | tf_op jit(solution)/shard_map/jit(cholesky)/cholesky | solution.py:31
  322.4 9.8 %custom-call.33 = f32[1,128,128]{1,2,0:T(8,128)S(1)} custom-call(f32[1,128,128]{2,1,0:T(8,128)S(1)} %get-tuple-element.24), custom_call_target="InvertDiagBlocksLowerTriangular" | custom-call | tf_op jit(solution)/shard_map/jit(cholesky)/cholesky | solution.py:31
  332.8 11.9 %cholesky.255 = f32[128,128]{1,0:T(8,128)S(1)} custom-call(f32[128,128]{1,0:T(8,128)S(1)} %convolution_subtract_fusion.4), custom_call_target="Cholesky" | custom-call | tf_op jit(solution)/shard_map/jit(cholesky)/cholesky | solution.py:31
  348.7 8.5 %while.1 = (s32[]{:T(128)}, f32[512,512]{1,0:T(8,128)S(1)}, s32[4,2]{0,1:T(2,128)S(1)}, f32[4,128,128]{2,1,0:T(8,128)S(1)}, s32[]{:T(128)}) while((s32[]{:T(128)}, f32[512,512]{1,0:T(8,128)S(1)}, s32[4,2]{0,1:T(2,128)S(1)}, f32[4,128,128]{2,1,0:T(8,128)S(1)}, s32[]{:T(128)}) %tuple.34), condition=%wide.while_cond, body=%wide.while_body.sunk | while | flops 2 | bytes 131181 | solution.py:32
  357.2 39.3 %custom-call.34 = f32[4,128,128]{1,2,0:T(8,128)S(1)} custom-call(f32[4,128,128]{2,1,0:T(8,128)S(1)} %get-tuple-element.10), custom_call_target="InvertDiagBlocksLowerTriangular" | custom-call | tf_op jit(solution)/shard_map/jit(_solve_triangular)/triangular_solve | solution.py:32
  398.9 2.8 convolution_subtract_fusion.1
  402.6 3.2 convolution_subtract_fusion
  406.8 4.7 fusion.9
  413.4 11.3 %fusion.41 = f32[2048,512]{1,0:T(8,128)} fusion(f32[1,1792,2048]{2,1,0:T(8,128)} %param.5, bf16[1,1792,2048]{2,1,0:T(8,128)(2,1)S(1)} %bitcast.69, bf16[128,1792]{1,0:T(8,128)(2,1)S(1)} %convolution_convert_fusion.1, bf16[128,1792]{1,0:T(8,128)(2,1)S(1)} %get-tuple-element.33, bf16[128,1792]{1,0:T(8,128)(2,1)S(1)} %get-tuple-element.35, ...), kind=kOutput, calls=%fused_computation.86 | convolution fusion | flops 3776446464 | bytes 28049408 | tf_op jit(solution)/shard_map/ij,ik->jk/dot_general | solution.py:34
  424.7 142.7 %all-reduce.6.cloned.1.call-done = f32[2048,512]{1,0:T(8,128)} async-done(((f32[2048,512]{1,0:T(8,128)}), f32[2048,512]{1,0:T(8,128)}) %all-reduce.6.cloned.1.call-update) | async-done | bytes 4194320 | tf_op jit(solution)/shard_map/psum | solution.py:37
  567.4 2.9 multiply_reduce_fusion
  572.0 8.2 %subtract_convert_fusion = bf16[1792,2048]{1,0:T(8,128)(2,1)} fusion(bf16[1792,2048]{1,0:T(8,128)(2,1)} %param.4, f32[2048,512]{1,0:T(8,128)S(1)} %multiply_divide_fusion, bf16[128,1792]{1,0:T(8,128)(2,1)S(1)} %copy-done.5, bf16[128,1792]{1,0:T(8,128)(2,1)S(1)} %copy-done.3, bf16[128,1792]{1,0:T(8,128)(2,1)S(1)} %get-tuple-element.35, ...), kind=kOutput, calls=%fused_computation.5 | convolution fusion | flops 3781165056 | bytes 20709376 | tf_op jit(solution)/shard_map/dot_general | solution.py:42
  581.3 13.0 %fusion = f32[1,1792,2048]{2,1,0:T(8,128)} fusion(f32[1,1792,2048]{2,1,0:T(8,128)} %param.5, bf16[1,1792,2048]{2,1,0:T(8,128)(2,1)} %param.6, f32[2048,512]{1,0:T(8,128)S(1)} %copy-done, bf16[128,1792]{1,0:T(8,128)(2,1)} %copy-done.4, bf16[128,1792]{1,0:T(8,128)(2,1)} %copy-done.2, bf16[128,1792]{1,0:T(8,128)(2,1)S(1)} %get-tuple-element.35, ...), kind=kOutput, calls=%fused_computation.4 | convolution fusion | flops 3782213632 | bytes 42729472 | tf_op jit(solution)/shard_map/dot_general | solution.py:39
  (68 shorter events, 27.6 us)
Async XLA Ops:
  7.2 41.2 %all-gather.4.cloned.1.call-start = ((), (), s32[]{:S(2)}) async-start(), calls=%async_computation | async-start | bytes 2621440 | tf_op jit(solution)/shard_map/all_gather | solution.py:22
  9.3 186.1 %all-gather.6.cloned.1.call-start = ((), (), s32[]{:S(2)}) async-start(), calls=%async_computation.3 | async-start | bytes 16515072 | tf_op jit(solution)/shard_map/all_gather | solution.py:27
  61.4 200.5 %all-reduce.4.cloned.1.call-start = ((), (), s32[]{:S(2)}) async-start(), calls=%async_computation.1 | async-start | bytes 2097152 | tf_op jit(solution)/shard_map/psum | solution.py:30
  211.2 356.3 %all-reduce.6.cloned.1.call-start = ((), (), s32[]{:S(2)}) async-start(), calls=%async_computation.2 | async-start | bytes 8388608 | tf_op jit(solution)/shard_map/psum | solution.py:37
  396.6 6.1 %copy-start.1 = (f32[512,1792]{0,1:T(8,128)S(1)}, f32[512,1792]{0,1:T(8,128)}, u32[]{:S(2)}) copy-start(f32[512,1792]{0,1:T(8,128)} %fusion.1) | copy-start | bytes 11010052
  401.7 11.8 %slice-start = ((s8[7340032]{0:T(1024)(128)(4,1)}), s8[4194304]{0:T(1024)(128)(4,1)S(1)}, s32[]{:S(2)}) async-start(s8[7340032]{0:T(1024)(128)(4,1)} %bitcast.68), calls=%async_computation.4 | async-start | bytes 8388608
  405.8 7.6 %slice-start.1 = ((s8[7340032]{0:T(1024)(128)(4,1)}), s8[3145728]{0:T(1024)(128)(4,1)S(1)}, s32[]{:S(2)}) async-start(s8[7340032]{0:T(1024)(128)(4,1)} %bitcast.68), calls=%async_computation.5 | async-start | bytes 6291456
  406.8 17.9 %copy-start.2 = (bf16[128,1792]{1,0:T(8,128)(2,1)}, bf16[128,1792]{1,0:T(8,128)(2,1)S(1)}, u32[]{:S(2)}) copy-start(bf16[128,1792]{1,0:T(8,128)(2,1)S(1)} %get-tuple-element.33) | copy-start | bytes 1376260
  412.7 0.8 copy-start.4
  567.4 3.4 copy-start
  570.9 1.0 copy-start.3
  570.9 1.2 copy-start.5
Sparse Core Ops, SparseCore 0:
  10.4 37.8 all-gather.3
  61.5 133.8 all-gather.5
  211.3 50.6 all-reduce.3
  424.9 142.5 all-reduce.5
